TPU v7x, 32 devices: a whole 2x2x4 slice. The times are simulated.
32 devices in a mesh: row: 8 (over y, x, core), col: 4 (over z).
Axes of the slice: x: 2, y: 2, z: 4, core: 2. Of those that a mesh axis runs over, the one named last changes fastest.
Arguments:
- gradient: bfloat16 [24576, 24576], P('row', 'col'), may hold values from -6 to 6
- sensitivity: bfloat16 [24576, 16384], P('row', 'col'), may hold values from -0.0390625 to 0.0390625
Outputs:
- influence: float32 [512, 16384], P('row', 'col')
All inputs are finite; a program needn't handle non-finite values.
Results may differ from a plain program's by a relative error of at most 0.0029.
Values may be sent and summed in bfloat16 or wider, within the bound.
A program may use at most 128 MiB of HBM per device.

v0:
```python
import jax
import jax.numpy as jnp
from jax import lax
from jax.sharding import PartitionSpec as P

PANEL = 512


def from_root(value, axis, root):
    mine = lax.axis_index(axis) == root
    return lax.psum(jnp.where(mine, value, jnp.zeros_like(value)), axis)


def shards(gradient, sensitivity):
    ratio = lax.axis_size("row") // lax.axis_size("col")
    own_panel = sensitivity[:, :PANEL]
    panel_here = from_root(own_panel, "col", 0)
    col_index = lax.axis_index("col")
    pieces = []
    for member in range(ratio):
        pieces.append(from_root(panel_here, "row", col_index * ratio + member))
    panel_block = jnp.concatenate(pieces, axis=0)
    partial_value = jnp.dot(gradient, panel_block, preferred_element_type=jnp.float32)
    image = lax.psum(partial_value, "col").astype(jnp.bfloat16)
    return lax.psum_scatter(
        lax.dot_general(
            image, sensitivity, (((0,), (0,)), ((), ())), preferred_element_type=jnp.float32
        ),
        "row",
        scatter_dimension=0,
        tiled=True,
    )


def solution(mesh):
    return jax.shard_map(
        shards,
        mesh=mesh,
        in_specs=(P("row", "col"), P("row", "col")),
        out_specs=P("row", "col"),
        check_vma=False,
    )
```

profile of v0, /device:TPU:0, one launch (start us, length us, event | category | flops | bytes accessed | tf_op | source)
XLA Modules:
  0.0 583.4 jit_solution(8317482870267149150)
XLA Ops:
  6.5 0.0 all-reduce.5.cloned.1.call-start
  6.5 3.8 slice_select_fusion
  10.3 0.0 all-reduce.5.cloned.1.call-update
  10.3 0.0 all-reduce.7.cloned.1.call-start
  10.4 123.9 %all-reduce.5.cloned.1.call-done = bf16[3072,512]{1,0:T(8,128)(2,1)} async-done(((bf16[3072,512]{1,0:T(8,128)(2,1)}), bf16[3072,512]{1,0:T(8,128)(2,1)}) %all-reduce.5.cloned.1.call-update) | async-done | bytes 3145744 | tf_op jit(solution)/shard_map/psum | solution.py:11
  134.3 5.0 broadcast_select_fusion.1
  139.2 0.0 all-reduce.7.cloned.1.call-update
  139.2 0.0 reduce-scatter.2.cloned.1.call-start
  139.3 103.5 %all-reduce.7.cloned.1.call-done = (bf16[3072,512]{1,0:T(8,128)(2,1)}, bf16[3072,512]{1,0:T(8,128)(2,1)}) async-done(((bf16[3072,512]{1,0:T(8,128)(2,1)}, bf16[3072,512]{1,0:T(8,128)(2,1)}), (bf16[3072,512]{1,0:T(8,128)(2,1)}, bf16[3072,512]{1,0:T(8,128)(2,1)})) %all-reduce.7.cloned.1.call-update) | async-done | bytes 6291472 | tf_op jit(solution)/shard_map/psum | solution.py:11
  242.8 27.1 %fusion.4 = f32[3072,512]{0,1:T(8,128)} fusion(bf16[3072,6144]{1,0:T(8,128)(2,1)} %param.2, bf16[3072,512]{1,0:T(8,128)(2,1)} %get-tuple-element.5, bf16[3072,512]{1,0:T(8,128)(2,1)} %get-tuple-element.6), kind=kOutput, calls=%fused_computation.4 | convolution fusion | flops 19339935744 | bytes 50331648 | tf_op jit(solution)/shard_map/dot_general | solution.py:23
  269.9 217.7 %all-reduce.8 = bf16[3072,512]{0,1:T(8,128)(2,1)S(1)} all-reduce(f32[3072,512]{0,1:T(8,128)} %fusion.4), channel_id=1, replica_groups=mesh['row'=8,'col'=4] {'col'}, use_global_device_ids=true, to_apply=%region_3.4 | all-reduce | flops 1572864 | bytes 9437184 | tf_op jit(solution)/shard_map/psum | solution.py:24
  487.5 19.9 %fusion.10 = f32[512,4096]{1,0:T(8,128)} fusion(bf16[3072,512]{0,1:T(8,128)(2,1)S(1)} %all-reduce.8, bf16[3072,4096]{1,0:T(8,128)(2,1)} %param.3), kind=kOutput, calls=%fused_computation.11 | convolution fusion | flops 12884901888 | bytes 36700160 | tf_op jit(solution)/shard_map/dot_general | solution.py:26
  507.4 0.0 reduce-scatter.2.cloned.1.call-update
  507.4 69.4 %reduce-scatter.2.cloned.1.call-done = f32[64,4096]{1,0:T(8,128)} async-done(((f32[512,4096]{1,0:T(8,128)}), f32[64,4096]{1,0:T(8,128)}) %reduce-scatter.2.cloned.1.call-update) | async-done | bytes 1048592 | tf_op jit(solution)/shard_map/reduce_scatter | solution.py:25
Async XLA Ops:
  6.5 127.7 %all-reduce.5.cloned.1.call-start = ((), (), s32[]{:S(2)}) async-start(), calls=%async_computation.1 | async-start | bytes 6291456 | tf_op jit(solution)/shard_map/psum | solution.py:11
  10.3 232.5 %all-reduce.7.cloned.1.call-start = ((), (), s32[]{:S(2)}) async-start(), calls=%async_computation.3 | async-start | bytes 12582912 | tf_op jit(solution)/shard_map/psum | solution.py:11
  139.2 437.6 %reduce-scatter.2.cloned.1.call-start = ((), (), s32[]{:S(2)}) async-start(), calls=%async_computation.2 | async-start | bytes 9437184 | tf_op jit(solution)/shard_map/reduce_scatter | solution.py:25
Sparse Core Ops, SparseCore 0:
  10.4 123.7 all-reduce.4
  139.4 103.3 all-reduce.6
  507.6 69.2 reduce-scatter.1
where the time goes:
time: 584 us; the launch traced here: 583 us
  waiting for transfers between devices  297 us (51%)
  blocking collectives  218 us (37%)
  matrix products  47 us (8%)
  between operations  13.1 us (2%)
  other arithmetic  8.71 us (1%)
    psum x2, waiting for transfers between devices, from_root(): return lax.psum(jnp.where(mine, value, jnp.zeros_like(value)), axis)  227 us
    psum x1, blocking collectives, shards(): image = lax.psum(partial_value, 'col').astype(jnp.bfloat16)  218 us
    reduce_scatter x1, waiting for transfers between devices, shards(): lax.psum_scatter(lax.dot_general(image, sensitivity, (((0,), (0,)), ((),...  69.4 us
    dot_general x1, matrix products, shards(): jnp.dot(gradient, panel_block, preferred_element_type=jnp.float32)  27.1 us
    dot_general x1, matrix products, shards(): lax.dot_general(image, sensitivity, (((0,), (0,)), ((), ())), preferred_e...  19.9 us
  transfers between devices with their start and end apart: 3, of which 3 were waited for; matrix products, arithmetic and copies ran while one was open for 0% of the time, Pallas kernels for 0%

commit v1 on v0

--- a/solution.py
+++ b/solution.py
@@ -21,7 +21,7 @@
         pieces.append(from_root(panel_here, "row", col_index * ratio + member))
     panel_block = jnp.concatenate(pieces, axis=0)
     partial_value = jnp.dot(gradient, panel_block, preferred_element_type=jnp.float32)
-    image = lax.psum(partial_value, "col").astype(jnp.bfloat16)
+    image = jnp.sum(lax.all_gather(partial_value, "col"), axis=0).astype(jnp.bfloat16)
     return lax.psum_scatter(
         lax.dot_general(
             image, sensitivity, (((0,), (0,)), ((), ())), preferred_element_type=jnp.float32

time: 584 us -> 840 us (1.44)
  waiting for transfers between devices: 297 us -> 722 us
  blocking collectives: 218 us -> 0 us
  local copies, waits for them, and re-layouts: 0 us -> 29.1 us
  other arithmetic: 8.71 us -> 27.6 us
    all_gather x0 -> x1, waiting for transfers between devices: none -> 425 us  [shards(): lax.all_gather(partial_value, 'col')]
    psum x1 -> x0, blocking collectives: 218 us -> none  [shards(): image = lax.psum(partial_value, 'col').astype(jnp.bfloat16)]
    all_gather x0 -> x1, local copies, waits for them, and re-layouts: none -> 29.1 us  [shards(): lax.all_gather(partial_value, 'col')]
    reduce_sum x0 -> x1, other arithmetic: none -> 18.9 us  [shards(): jnp.sum(lax.all_gather(partial_value, 'col'), axis=0).astype(jnp.bfloat16)]
  transfers between devices with their start and end apart: 3 -> 4, of which waited for: 3 -> 4; matrix products, arithmetic and copies ran while one was open for 0% -> 0% of each run, Pallas kernels for 0% -> 0%
where the time goes in v1:
time: 840 us; the launch traced here: 839 us
  waiting for transfers between devices  722 us (86%)
  matrix products  46.9 us (6%)
  local copies, waits for them, and re-layouts  29.1 us (3%)
  other arithmetic  27.6 us (3%)
  between operations  13.1 us (2%)
    all_gather x1, waiting for transfers between devices, shards(): lax.all_gather(partial_value, 'col')  425 us
    psum x2, waiting for transfers between devices, from_root(): return lax.psum(jnp.where(mine, value, jnp.zeros_like(value)), axis)  227 us
    reduce_scatter x1, waiting for transfers between devices, shards(): lax.psum_scatter(lax.dot_general(image, sensitivity, (((0,), (0,)), ((),...  69.6 us
    all_gather x1, local copies, waits for them, and re-layouts, shards(): lax.all_gather(partial_value, 'col')  29.1 us
    dot_general x1, matrix products, shards(): jnp.dot(gradient, panel_block, preferred_element_type=jnp.float32)  27 us
    dot_general x1, matrix products, shards(): lax.dot_general(image, sensitivity, (((0,), (0,)), ((), ())), preferred_e...  19.9 us
    reduce_sum x1, other arithmetic, shards(): jnp.sum(lax.all_gather(partial_value, 'col'), axis=0).astype(jnp.bfloat16)  18.9 us
  transfers between devices with their start and end apart: 4, of which 4 were waited for; matrix products, arithmetic and copies ran while one was open for 0% of the time, Pallas kernels for 0%

profile of v1, /device:TPU:0, one launch (start us, length us, event | category | flops | bytes accessed | tf_op | source)
XLA Modules:
  0.0 839.2 jit_solution(9607087568853091443)
XLA Ops:
  6.5 0.0 all-reduce.4.cloned.1.call-start
  6.5 3.8 slice_select_fusion
  10.3 0.0 all-reduce.4.cloned.1.call-update
  10.3 0.0 all-reduce.6.cloned.1.call-start
  10.4 123.9 %all-reduce.4.cloned.1.call-done = bf16[3072,512]{1,0:T(8,128)(2,1)} async-done(((bf16[3072,512]{1,0:T(8,128)(2,1)}), bf16[3072,512]{1,0:T(8,128)(2,1)}) %all-reduce.4.cloned.1.call-update) | async-done | bytes 3145744 | tf_op jit(solution)/shard_map/psum | solution.py:11
  134.3 5.0 broadcast_select_fusion.1
  139.2 0.0 all-reduce.6.cloned.1.call-update
  139.2 0.0 all-gather.3.cloned.1.call-start
  139.3 103.5 %all-reduce.6.cloned.1.call-done = (bf16[3072,512]{1,0:T(8,128)(2,1)}, bf16[3072,512]{1,0:T(8,128)(2,1)}) async-done(((bf16[3072,512]{1,0:T(8,128)(2,1)}, bf16[3072,512]{1,0:T(8,128)(2,1)}), (bf16[3072,512]{1,0:T(8,128)(2,1)}, bf16[3072,512]{1,0:T(8,128)(2,1)})) %all-reduce.6.cloned.1.call-update) | async-done | bytes 6291472 | tf_op jit(solution)/shard_map/psum | solution.py:11
  242.8 27.0 %fusion.4 = f32[3072,512]{0,1:T(8,128)} fusion(bf16[3072,6144]{1,0:T(8,128)(2,1)} %param.2, bf16[3072,512]{1,0:T(8,128)(2,1)} %get-tuple-element.5, bf16[3072,512]{1,0:T(8,128)(2,1)} %get-tuple-element.6), kind=kOutput, calls=%fused_computation.4 | convolution fusion | flops 19339935744 | bytes 50331648 | tf_op jit(solution)/shard_map/dot_general | solution.py:23
  269.8 0.0 all-gather.3.cloned.1.call-update
  269.8 0.2 reduce-scatter.2.cloned.1.call-start
  270.1 425.1 %all-gather.3.cloned.1.call-done = f32[12288,512]{0,1:T(8,128)} async-done(((f32[3072,512]{0,1:T(8,128)}), f32[12288,512]{0,1:T(8,128)}) %all-gather.3.cloned.1.call-update) | async-done | bytes 25165840 | tf_op jit(solution)/shard_map/all_gather | solution.py:24
  695.2 29.1 %reshape = f32[4,3072,512]{1,0,2:T(4,128)} reshape(f32[12288,512]{0,1:T(8,128)} %all-gather.3.cloned.1.call-done) | data formatting | bytes 50331648 | tf_op jit(solution)/shard_map/all_gather | solution.py:24
  724.3 18.9 %reduce_sum.9 = bf16[3072,512]{0,1:T(8,128)(2,1)S(1)} reduce(f32[4,3072,512]{1,0,2:T(4,128)} %reshape, f32[]{:T(128)} %constant.18.clone.1), dimensions={0}, to_apply=%region_3.4 | reduce | flops 4718592 | bytes 28311556 | tf_op jit(solution)/shard_map/reduce_sum | solution.py:24
  743.2 19.9 %fusion.10 = f32[512,4096]{1,0:T(8,128)} fusion(bf16[3072,512]{0,1:T(8,128)(2,1)S(1)} %reduce_sum.9, bf16[3072,4096]{1,0:T(8,128)(2,1)} %param.3), kind=kOutput, calls=%fused_computation.11 | convolution fusion | flops 12884901888 | bytes 36700160 | tf_op jit(solution)/shard_map/dot_general | solution.py:26
  763.0 0.0 reduce-scatter.2.cloned.1.call-update
  763.1 69.6 %reduce-scatter.2.cloned.1.call-done = f32[64,4096]{1,0:T(8,128)} async-done(((f32[512,4096]{1,0:T(8,128)}), f32[64,4096]{1,0:T(8,128)}) %reduce-scatter.2.cloned.1.call-update) | async-done | bytes 1048592 | tf_op jit(solution)/shard_map/reduce_scatter | solution.py:25
Async XLA Ops:
  6.5 127.7 %all-reduce.4.cloned.1.call-start = ((), (), s32[]{:S(2)}) async-start(), calls=%async_computation.1 | async-start | bytes 6291456 | tf_op jit(solution)/shard_map/psum | solution.py:11
  10.3 232.5 %all-reduce.6.cloned.1.call-start = ((), (), s32[]{:S(2)}) async-start(), calls=%async_computation.4 | async-start | bytes 12582912 | tf_op jit(solution)/shard_map/psum | solution.py:11
  139.2 556.0 %all-gather.3.cloned.1.call-start = ((), (), s32[]{:S(2)}) async-start(), calls=%async_computation.3 | async-start | bytes 31457280 | tf_op jit(solution)/shard_map/all_gather | solution.py:24
  269.8 562.9 %reduce-scatter.2.cloned.1.call-start = ((), (), s32[]{:S(2)}) async-start(), calls=%async_computation.2 | async-start | bytes 9437184 | tf_op jit(solution)/shard_map/reduce_scatter | solution.py:25
Sparse Core Ops, SparseCore 0:
  10.4 123.7 all-reduce.3
  139.4 103.3 all-reduce.5
  269.9 425.2 all-gather.2
  763.2 69.4 reduce-scatter.1
